TPU v7x, 512 devices: a whole 4x4x16 slice. The times are simulated.
512 devices in a mesh: samp: 128 (over z, y, core), cell: 4 (over x).
Axes of the slice: x: 4, y: 4, z: 16, core: 2. Of those that a mesh axis runs over, the one named last changes fastest.
Arguments:
- points: float32 [24, 262144], P(None, 'samp'), may hold values from -1 to 1
- yields: bfloat16 [262144, 1024], P('samp', 'cell'), may hold values from -6 to 6
- term_index: int32 [512, 2], replicated, may hold values from 0 to 95, as said below
- block_group: int32 [8], replicated, may hold values from 0 to 7
Outputs:
- coefficients: float32 [512, 1024], P('cell')
- sobol: float32 [8, 1024], P(None, 'cell')
Inputs may be any that keep to these rules, and one draw needn't show every extreme that they name: `term_index`: row 0 is 0, 0 (the constant term); every other row names one parameter with degree 1 to 3 and column 0, or two different parameters with degrees 1 to 3 each, the lower column first; no two rows are the same.
All inputs are finite; a program needn't handle non-finite values.
Results may differ from a plain program's by a relative error of at most 0.0037.
Values sent between devices are 32-bit elements; how exact they have to be, the bound alone decides.
A program may use at most 64 MiB of HBM per device.

v0:
```python
import jax
import jax.numpy as jnp
from jax import lax
from jax.sharding import PartitionSpec as P

BLOCK = 64
GROUPS = 8


def basis_rows(xs):
    ones = jnp.ones_like(xs)
    first = 1.7320508075688772 * xs
    second = 2.23606797749979 * (1.5 * xs * xs - 0.5)
    third = 2.6457513110645907 * (2.5 * xs * xs * xs - 1.5 * xs)
    stacked = jnp.stack([ones, first, second, third], axis=1)
    return stacked.reshape(4 * xs.shape[0], xs.shape[1])


def design(xs, term_index):
    table = basis_rows(xs)
    left = jnp.take(table, term_index[:, 0], axis=0)
    right = jnp.take(table, term_index[:, 1], axis=0)
    return (left * right).astype(jnp.bfloat16)


def on_device(points, yields, term_index, block_group):
    psi = design(points, term_index)
    cross_local = jnp.dot(psi, yields, preferred_element_type=jnp.float32)
    gram_local = jnp.dot(psi, psi.T, preferred_element_type=jnp.float32)
    gram, cross = lax.psum((gram_local, cross_local), "samp")
    lower = jnp.linalg.cholesky(gram)
    inner = lax.linalg.triangular_solve(lower, cross, left_side=True, lower=True)
    coef = lax.linalg.triangular_solve(lower, inner, left_side=True, lower=True, transpose_a=True)
    total_samples = points.shape[1] * lax.axis_size("samp")
    scaled = coef * jnp.sqrt(jnp.float32(total_samples))
    terms = coef.shape[0]
    keep = (jnp.arange(terms) >= 1).astype(jnp.float32)
    squares = coef * coef * keep[:, None]
    groups = jnp.repeat(block_group, BLOCK)
    member = (groups[None, :] == jnp.arange(GROUPS, dtype=jnp.int32)[:, None]).astype(jnp.float32)
    part = jnp.dot(member, squares, precision=lax.Precision.HIGHEST)
    total = jnp.sum(squares, axis=0)
    sobol = part / total[None, :]
    coefficients = lax.all_to_all(scaled, "cell", split_axis=0, concat_axis=1, tiled=True)
    return (coefficients, sobol)


def solution(mesh):
    placed = (P(None, "samp"), P("samp", "cell"), P(), P())
    return jax.shard_map(
        on_device,
        mesh=mesh,
        in_specs=placed,
        out_specs=(P("cell", None), P(None, "cell")),
        check_vma=False,
    )
```

profile of v0, /device:TPU:8, one launch (start us, length us, event | category | flops | bytes accessed | tf_op | source)
XLA Modules:
  0.0 542.7 jit_solution(15287291031429529462)
XLA Ops:
  7.2 0.8 fusion.59
  8.0 1.0 multiply_bitcast_fusion
  9.2 0.5 copy.6
  10.0 3.6 gather_fusion
  13.6 3.6 gather_fusion.1
  17.2 4.0 fusion
  21.2 2.3 fusion.60
  23.6 1.5 fusion.61
  25.1 350.2 %all-reduce.4.cloned.1.call-done = (f32[512,256]{1,0:T(8,128)}, f32[512,512]{0,1:T(8,128)}) async-done(((f32[512,256]{1,0:T(8,128)}, f32[512,512]{0,1:T(8,128)}), (f32[512,256]{1,0:T(8,128)}, f32[512,512]{0,1:T(8,128)})) %all-reduce.4.cloned.1.call-update) | async-done | bytes 1572880 | tf_op jit(solution)/shard_map/psum | solution.py:30
  375.3 1.6 copy.8
  376.8 1.5 fusion.1
  378.3 11.7 %cholesky.104 = f32[128,128]{1,0:T(8,128)S(1)} custom-call(f32[128,128]{1,0:T(8,128)S(1)} %cholesky.266), custom_call_target="Cholesky" | custom-call | tf_op jit(solution)/shard_map/jit(cholesky)/cholesky | solution.py:31
  390.2 9.8 %custom-call.32 = f32[1,128,128]{1,2,0:T(8,128)S(1)} custom-call(f32[1,128,128]{2,1,0:T(8,128)S(1)} %get-tuple-element.37), custom_call_target="InvertDiagBlocksLowerTriangular" | custom-call | tf_op jit(solution)/shard_map/jit(cholesky)/cholesky | solution.py:31
  400.0 0.3 constant_dynamic-update-slice_fusion.3
  400.3 0.3 convolution_subtract_fusion
  400.7 11.9 %cholesky.217 = f32[128,128]{1,0:T(8,128)S(1)} custom-call(f32[128,128]{1,0:T(8,128)S(1)} %cholesky.270), custom_call_target="Cholesky" | custom-call | tf_op jit(solution)/shard_map/jit(cholesky)/cholesky | solution.py:31
  412.6 0.7 compare_reduce_fusion.2
  413.3 0.6 compare_reduce_fusion.3
  414.0 9.8 %custom-call.33 = f32[1,128,128]{1,2,0:T(8,128)S(1)} custom-call(f32[1,128,128]{2,1,0:T(8,128)S(1)} %get-tuple-element.34), custom_call_target="InvertDiagBlocksLowerTriangular" | custom-call | tf_op jit(solution)/shard_map/jit(cholesky)/cholesky | solution.py:31
  424.1 0.4 convolution_subtract_fusion.5
  424.5 11.7 %cholesky.238 = f32[128,128]{1,0:T(8,128)S(1)} custom-call(f32[128,128]{1,0:T(8,128)S(1)} %cholesky.275), custom_call_target="Cholesky" | custom-call | tf_op jit(solution)/shard_map/jit(cholesky)/cholesky | solution.py:31
  436.2 0.6 compare_reduce_fusion.1
  436.8 9.8 %custom-call.34 = f32[1,128,128]{1,2,0:T(8,128)S(1)} custom-call(f32[1,128,128]{2,1,0:T(8,128)S(1)} %get-tuple-element.31), custom_call_target="InvertDiagBlocksLowerTriangular" | custom-call | tf_op jit(solution)/shard_map/jit(cholesky)/cholesky | solution.py:31
  446.9 0.4 convolution_subtract_fusion.8
  447.3 11.9 %cholesky.255 = f32[128,128]{1,0:T(8,128)S(1)} custom-call(f32[128,128]{1,0:T(8,128)S(1)} %convolution_subtract_fusion.8), custom_call_target="Cholesky" | custom-call | tf_op jit(solution)/shard_map/jit(cholesky)/cholesky | solution.py:31
  459.2 0.7 compare_reduce_fusion
  462.6 10.9 %while.1 = (s32[]{:T(128)}, f32[512,512]{1,0:T(8,128)S(1)}, s32[4,2]{0,1:T(2,128)S(1)}, f32[4,128,128]{2,1,0:T(8,128)}, s32[]{:T(128)}) while((s32[]{:T(128)}, f32[512,512]{1,0:T(8,128)S(1)}, s32[4,2]{0,1:T(2,128)S(1)}, f32[4,128,128]{2,1,0:T(8,128)}, s32[]{:T(128)}) %tuple.36), condition=%wide.while_cond, body=%wide.while_body.sunk | while | flops 2 | bytes 132705 | solution.py:33
  462.7 0.6 fusion.77
  463.3 2.0 bitcast_dynamic-update-slice_fusion.2
  465.4 0.6 fusion.77
  466.0 2.0 bitcast_dynamic-update-slice_fusion.2
  468.1 0.6 fusion.77
  468.7 2.0 bitcast_dynamic-update-slice_fusion.2
  470.8 0.6 fusion.77
  471.4 2.1 bitcast_dynamic-update-slice_fusion.2
  473.5 40.1 %custom-call.35 = f32[4,128,128]{1,2,0:T(8,128)S(1)} custom-call(f32[4,128,128]{2,1,0:T(8,128)} %get-tuple-element.10), custom_call_target="InvertDiagBlocksLowerTriangular" | custom-call | tf_op jit(solution)/shard_map/triangular_solve | solution.py:33
  513.6 1.2 fusion.33
  514.8 1.2 convolution_subtract_fusion.7
  516.0 0.3 fusion.46
  516.3 1.2 convolution_subtract_fusion.4
  517.8 1.3 convolution_subtract_fusion.3
  520.3 0.4 convolution_subtract_fusion.2
  521.0 0.5 convolution_subtract_fusion.1
  521.8 0.9 fusion.2
  522.6 4.3 all-to-all-start
  527.0 1.0 convolution_divide_fusion
  528.0 7.0 %all-to-all-done = f32[4,128,256]{2,1,0:T(8,128)S(1)} async-done(((f32[4,128,256]{2,1,0:T(8,128)}), f32[4,128,256]{2,1,0:T(8,128)S(1)}, u32[]{:S(2)}, u32[]{:S(2)}) %all-to-all-start) | async-done | bytes 524320 | tf_op jit(solution)/shard_map/all_to_all | solution.py:44
  535.0 0.8 copy.11
  (42 shorter events, 3.8 us)
Async XLA Ops:
  7.2 16.4 %copy-start = (bf16[2048,256]{1,0:T(8,128)(2,1)S(1)}, bf16[2048,256]{1,0:T(8,128)(2,1)}, u32[]{:S(2)}) copy-start(bf16[2048,256]{1,0:T(8,128)(2,1)} %param.7) | copy-start | bytes 3145732
  7.2 368.1 %all-reduce.4.cloned.1.call-start = ((), (), s32[]{:S(2)}) async-start(), calls=%async_computation.1 | async-start | bytes 3145728 | tf_op jit(solution)/shard_map/psum | solution.py:30
  514.8 12.1 %copy-start.1 = (s32[8]{0:T(128)S(1)}, s32[8]{0:T(128)}, u32[]{:S(2)}) copy-start(s32[8]{0:T(128)} %param.9) | copy-start | bytes 100
  522.6 12.3 %all-to-all-start = ((f32[4,128,256]{2,1,0:T(8,128)}), f32[4,128,256]{2,1,0:T(8,128)S(1)}, u32[]{:S(2)}, u32[]{:S(2)}) async-start(f32[4,128,256]{2,1,0:T(8,128)} %bitcast.16), calls=%async_computation | async-start | bytes 1048576 | tf_op jit(solution)/shard_map/all_to_all | solution.py:44
Sparse Core Ops, SparseCore 0:
  25.2 350.0 all-reduce.3
where the time goes:
time: 543 us
  waiting for transfers between devices  357 us (66%)
  other arithmetic  127 us (23%)
  local copies, waits for them, and re-layouts  22.3 us (4%)
  between operations  16.9 us (3%)
  matrix products  14.7 us (3%)
    psum x1, waiting for transfers between devices, on_device(): gram, cross = lax.psum((gram_local, cross_local), 'samp')  350 us
    another operation x15, other arithmetic, on_device(): lower = jnp.linalg.cholesky(gram)  79.5 us
    another operation x3, other arithmetic, on_device(): lax.linalg.triangular_solve(lower, inner, left_side=True, lower=True, tra...  40.3 us
    another operation x12, local copies, waits for them, and re-layouts  10.9 us
  transfers between devices with their start and end apart: 2, of which 2 were waited for; matrix products, arithmetic and copies ran while one was open for 0% of the time, Pallas kernels for 0%

commit v1 on v0

--- a/solution.py
+++ b/solution.py
@@ -41,7 +41,10 @@
     part = jnp.dot(member, squares, precision=lax.Precision.HIGHEST)
     total = jnp.sum(squares, axis=0)
     sobol = part / total[None, :]
-    coefficients = lax.all_to_all(scaled, "cell", split_axis=0, concat_axis=1, tiled=True)
+    coefficients = jnp.concatenate(
+        lax.all_to_all(jnp.stack(jnp.split(scaled, lax.axis_size("cell"), axis=0)), "cell", 0, 0),
+        axis=1,
+    )
     return (coefficients, sobol)
 
 

time: 543 us -> 547 us (level)
  no operation moved by 1% of the time
where the time goes in v1:
time: 547 us; the launch traced here: 543 us
  waiting for transfers between devices  357 us (65%)
  other arithmetic  128 us (23%)
  local copies, waits for them, and re-layouts  22.9 us (4%)
  between operations  17.1 us (3%)
  matrix products  14.7 us (3%)
    psum x1, waiting for transfers between devices, on_device(): gram, cross = lax.psum((gram_local, cross_local), 'samp')  350 us
    another operation x15, other arithmetic, on_device(): lower = jnp.linalg.cholesky(gram)  79.7 us
    another operation x3, other arithmetic, on_device(): lax.linalg.triangular_solve(lower, inner, left_side=True, lower=True, tra...  40.3 us
  transfers between devices with their start and end apart: 2, of which 2 were waited for; matrix products, arithmetic and copies ran while one was open for 0% of the time, Pallas kernels for 0%

profile of v1, /device:TPU:8, one launch (start us, length us, event | category | flops | bytes accessed | tf_op | source)
XLA Modules:
  0.0 543.3 jit_solution(17221552858641622813)
XLA Ops:
  7.2 0.8 fusion.59
  8.0 1.0 multiply_bitcast_fusion
  9.2 0.5 copy.9
  10.0 3.6 gather_fusion
  13.6 3.8 gather_fusion.1
  17.4 4.0 fusion
  21.5 2.3 fusion.60
  23.8 1.5 fusion.61
  25.4 349.6 %all-reduce.4.cloned.1.call-done = (f32[512,256]{1,0:T(8,128)}, f32[512,512]{0,1:T(8,128)}) async-done(((f32[512,256]{1,0:T(8,128)}, f32[512,512]{0,1:T(8,128)}), (f32[512,256]{1,0:T(8,128)}, f32[512,512]{0,1:T(8,128)})) %all-reduce.4.cloned.1.call-update) | async-done | bytes 1572880 | tf_op jit(solution)/shard_map/psum | solution.py:30
  375.0 1.6 copy.11
  376.6 1.5 fusion.1
  378.1 11.7 %cholesky.104 = f32[128,128]{1,0:T(8,128)S(1)} custom-call(f32[128,128]{1,0:T(8,128)S(1)} %cholesky.266), custom_call_target="Cholesky" | custom-call | tf_op jit(solution)/shard_map/jit(cholesky)/cholesky | solution.py:31
  389.9 9.8 %custom-call.32 = f32[1,128,128]{1,2,0:T(8,128)S(1)} custom-call(f32[1,128,128]{2,1,0:T(8,128)S(1)} %get-tuple-element.43), custom_call_target="InvertDiagBlocksLowerTriangular" | custom-call | tf_op jit(solution)/shard_map/jit(cholesky)/cholesky | solution.py:31
  399.8 0.3 constant_dynamic-update-slice_fusion.3
  400.1 0.3 convolution_subtract_fusion
  400.4 12.2 %cholesky.217 = f32[128,128]{1,0:T(8,128)S(1)} custom-call(f32[128,128]{1,0:T(8,128)S(1)} %cholesky.270), custom_call_target="Cholesky" | custom-call | tf_op jit(solution)/shard_map/jit(cholesky)/cholesky | solution.py:31
  412.6 0.7 compare_reduce_fusion.2
  413.3 0.6 compare_reduce_fusion.3
  414.0 9.8 %custom-call.33 = f32[1,128,128]{1,2,0:T(8,128)S(1)} custom-call(f32[1,128,128]{2,1,0:T(8,128)S(1)} %get-tuple-element.40), custom_call_target="InvertDiagBlocksLowerTriangular" | custom-call | tf_op jit(solution)/shard_map/jit(cholesky)/cholesky | solution.py:31
  424.0 0.4 convolution_subtract_fusion.5
  424.5 11.7 %cholesky.238 = f32[128,128]{1,0:T(8,128)S(1)} custom-call(f32[128,128]{1,0:T(8,128)S(1)} %cholesky.275), custom_call_target="Cholesky" | custom-call | tf_op jit(solution)/shard_map/jit(cholesky)/cholesky | solution.py:31
  436.2 0.6 compare_reduce_fusion.1
  436.8 9.8 %custom-call.34 = f32[1,128,128]{1,2,0:T(8,128)S(1)} custom-call(f32[1,128,128]{2,1,0:T(8,128)S(1)} %get-tuple-element.37), custom_call_target="InvertDiagBlocksLowerTriangular" | custom-call | tf_op jit(solution)/shard_map/jit(cholesky)/cholesky | solution.py:31
  446.9 0.4 convolution_subtract_fusion.8
  447.2 11.9 %cholesky.255 = f32[128,128]{1,0:T(8,128)S(1)} custom-call(f32[128,128]{1,0:T(8,128)S(1)} %convolution_subtract_fusion.8), custom_call_target="Cholesky" | custom-call | tf_op jit(solution)/shard_map/jit(cholesky)/cholesky | solution.py:31
  459.2 0.7 compare_reduce_fusion
  462.5 10.9 %while.1 = (s32[]{:T(128)}, f32[512,512]{1,0:T(8,128)S(1)}, s32[4,2]{0,1:T(2,128)S(1)}, f32[4,128,128]{2,1,0:T(8,128)}, s32[]{:T(128)}) while((s32[]{:T(128)}, f32[512,512]{1,0:T(8,128)S(1)}, s32[4,2]{0,1:T(2,128)S(1)}, f32[4,128,128]{2,1,0:T(8,128)}, s32[]{:T(128)}) %tuple.40), condition=%wide.while_cond, body=%wide.while_body.sunk | while | flops 2 | bytes 132705 | solution.py:33
  462.6 0.6 fusion.77
  463.2 2.0 bitcast_dynamic-update-slice_fusion.2
  465.3 0.6 fusion.77
  465.9 2.0 bitcast_dynamic-update-slice_fusion.2
  468.0 0.6 fusion.77
  468.6 2.0 bitcast_dynamic-update-slice_fusion.2
  470.7 0.6 fusion.77
  471.3 2.1 bitcast_dynamic-update-slice_fusion.2
  473.4 40.1 %custom-call.35 = f32[4,128,128]{1,2,0:T(8,128)S(1)} custom-call(f32[4,128,128]{2,1,0:T(8,128)} %get-tuple-element.10), custom_call_target="InvertDiagBlocksLowerTriangular" | custom-call | tf_op jit(solution)/shard_map/triangular_solve | solution.py:33
  513.5 1.2 fusion.33
  514.7 1.2 convolution_subtract_fusion.7
  516.2 1.2 convolution_subtract_fusion.4
  517.8 1.3 convolution_subtract_fusion.3
  519.1 0.3 fusion.50
  520.2 0.4 convolution_subtract_fusion.2
  520.9 0.5 convolution_subtract_fusion.1
  521.9 0.8 pad_maximum_fusion.2
  522.7 4.2 all-to-all-start
  527.1 1.0 convolution_divide_fusion
  528.1 7.0 %all-to-all-done = f32[4,128,256]{2,1,0:T(8,128)S(1)} async-done(((f32[4,128,256]{2,1,0:T(8,128)}), f32[4,128,256]{2,1,0:T(8,128)S(1)}, u32[]{:S(2)}, u32[]{:S(2)}) %all-to-all-start) | async-done | bytes 524320 | tf_op jit(solution)/shard_map/all_to_all | solution.py:45
  535.2 1.0 copy.13
  (45 shorter events, 4.2 us)
Async XLA Ops:
  7.2 16.6 %copy-start = (bf16[2048,256]{1,0:T(8,128)(2,1)S(1)}, bf16[2048,256]{1,0:T(8,128)(2,1)}, u32[]{:S(2)}) copy-start(bf16[2048,256]{1,0:T(8,128)(2,1)} %param.7) | copy-start | bytes 3145732
  7.2 367.8 %all-reduce.4.cloned.1.call-start = ((), (), s32[]{:S(2)}) async-start(), calls=%async_computation.1 | async-start | bytes 3145728 | tf_op jit(solution)/shard_map/psum | solution.py:30
  517.7 9.2 %copy-start.1 = (s32[8]{0:T(128)S(1)}, s32[8]{0:T(128)}, u32[]{:S(2)}) copy-start(s32[8]{0:T(128)} %param.9) | copy-start | bytes 100
  522.7 12.3 %all-to-all-start = ((f32[4,128,256]{2,1,0:T(8,128)}), f32[4,128,256]{2,1,0:T(8,128)S(1)}, u32[]{:S(2)}, u32[]{:S(2)}) async-start(f32[4,128,256]{2,1,0:T(8,128)} %pad_maximum_fusion.2), calls=%async_computation | async-start | bytes 1048576 | tf_op jit(solution)/shard_map/all_to_all | solution.py:45
Sparse Core Ops, SparseCore 0:
  25.5 349.4 all-reduce.3
